TPU v7x, 256 devices: a whole 4x4x8 slice. The times are simulated.
256 devices in a mesh: dp: 16 (over y_lo, z), expert: 16 (over y_hi, x, core).
Axes of the slice: x: 4, y: 4 (y_hi: 2, y_lo: 2; y = y_hi * 2 + y_lo), z: 8, core: 2. Of those that a mesh axis runs over, the one named last changes fastest.
Arguments:
- tokens: bfloat16 [32768, 2560], P(('dp', 'expert')), may hold values from -6 to 6
- routing: int32 [32768, 6], P(('dp', 'expert')), may hold values from 0 to 15, as said below
- gates: float32 [32768, 6], P(('dp', 'expert')), may hold values from 0.1 to 1
- cotangent: bfloat16 [32768, 2560], P(('dp', 'expert')), may hold values from -0.29882812 to 0.29882812
- w_in: bfloat16 [16, 2560, 768], P('expert'), may hold values from -0.125 to 0.125
- w_out: bfloat16 [16, 768, 2560], P('expert'), may hold values from -0.21875 to 0.21875
Outputs:
- grad_in: float32 [16, 2560, 768], P('expert', 'dp')
- grad_out: float32 [16, 768, 2560], P('expert', 'dp')
Inputs may be any that keep to these rules, and one draw needn't show every extreme that they name: `routing`: each row names 6 different experts.
All inputs are finite; a program needn't handle non-finite values.
Results may differ from a plain program's by a relative error of at most 0.0055.
Values may be sent and summed in bfloat16 or wider, within the bound.
A program may use at most 128 MiB of HBM per device.

v0:
```python
import jax
import jax.numpy as jnp
from jax import lax
from jax.sharding import PartitionSpec as P


def shifted(x, axis, by):
    devices = lax.axis_size(axis)
    return lax.ppermute(x, axis, [(i, (i + by) % devices) for i in range(devices)])


def silu_slope(values):
    sigma = jax.nn.sigmoid(values)
    return sigma * (1.0 + values * (1.0 - sigma))


def forward_rows(rows_in, weight_in):
    pre_act = jnp.dot(rows_in, weight_in, preferred_element_type=jnp.float32)
    return (pre_act, jax.nn.silu(pre_act).astype(jnp.bfloat16))


def backward_rows(rows_grad, weight_out, pre_act):
    back_grad = lax.dot_general(
        rows_grad, weight_out, (((1,), (1,)), ((), ())), preferred_element_type=jnp.float32
    )
    return (back_grad * silu_slope(pre_act)).astype(jnp.bfloat16)


def outer_sums(rows_in, rows_grad, hidden, pre_grad):
    grad_o = lax.dot_general(
        hidden, rows_grad, (((0,), (0,)), ((), ())), preferred_element_type=jnp.float32
    )
    grad_i = lax.dot_general(
        rows_in, pre_grad, (((0,), (0,)), ((), ())), preferred_element_type=jnp.float32
    )
    return (grad_i, grad_o)


def body(tokens, routing, gates, cotangent, w_in, w_out):
    peer_count = lax.axis_size("expert")
    half_axis = peer_count // 2
    tok_count = tokens.shape[0]
    top_count = routing.shape[1]
    width_model = tokens.shape[1]
    hidden_width = w_in.shape[2]
    entries = tok_count * top_count
    capacity = tok_count * top_count * 5 // (peer_count * 6)
    lend_rows = max(1, capacity * 2 // 5)
    own_slots = capacity - lend_rows
    chosen = routing.reshape(entries)
    onehot = (chosen[:, None] == jnp.arange(peer_count, dtype=jnp.int32)[None, :]).astype(jnp.int32)
    earlier = jnp.cumsum(onehot, axis=0) - onehot
    rank_of = jnp.sum(earlier * onehot, axis=1)
    spilled = rank_of >= own_slots
    target_device = jnp.where(spilled, (chosen + half_axis) % peer_count, chosen)
    target = jnp.where(
        rank_of < capacity, target_device * capacity + rank_of, peer_count * capacity
    )
    slot_entry = jnp.full((peer_count * capacity,), entries, jnp.int32)
    slot_entry = slot_entry.at[target].set(jnp.arange(entries, dtype=jnp.int32), mode="drop")
    token_of = slot_entry // top_count
    padded_tokens = jnp.concatenate([tokens, jnp.zeros((1, width_model), tokens.dtype)], axis=0)
    padded_cots = jnp.concatenate([cotangent, jnp.zeros((1, width_model), cotangent.dtype)], axis=0)
    padded_gates = jnp.concatenate([gates.reshape(entries), jnp.zeros((1,), jnp.float32)], axis=0)
    sent_inputs = padded_tokens[token_of].reshape(peer_count, capacity, width_model)
    sent_grads = (
        padded_cots[token_of].astype(jnp.float32) * padded_gates[slot_entry][:, None]
    ).astype(jnp.bfloat16)
    sent_grads = sent_grads.reshape(peer_count, capacity, width_model)
    weight_in = w_in[0]
    weight_out = w_out[0]
    got_inputs, got_grads = (
        lax.all_to_all(sent_inputs, "expert", split_axis=0, concat_axis=0, tiled=True),
        lax.all_to_all(sent_grads, "expert", split_axis=0, concat_axis=0, tiled=True),
    )
    own_count = peer_count * own_slots
    rows_in = got_inputs[:, :own_slots, :].reshape(own_count, width_model)
    rows_grad = got_grads[:, :own_slots, :].reshape(own_count, width_model)
    pre_act, hidden = forward_rows(rows_in, weight_in)
    pre_grad = backward_rows(rows_grad, weight_out, pre_act)
    part_in, part_out = outer_sums(rows_in, rows_grad, hidden, pre_grad)
    lend_inputs = got_inputs[:, own_slots:, :].reshape(peer_count * lend_rows, width_model)
    lend_grads = got_grads[:, own_slots:, :].reshape(peer_count * lend_rows, width_model)
    lent_in, lent_out = shifted((weight_in, weight_out), "expert", half_axis)
    lend_pre, lend_hidden = forward_rows(lend_inputs, lent_in)
    lend_pregrad = backward_rows(lend_grads, lent_out, lend_pre)
    far_inputs, far_grads, far_hidden, far_pregrad = shifted(
        (lend_inputs, lend_grads, lend_hidden, lend_pregrad), "expert", half_axis
    )
    extra_in, extra_out = outer_sums(far_inputs, far_grads, far_hidden, far_pregrad)
    rounded_in = (part_in + extra_in).astype(jnp.bfloat16)
    rounded_out = (part_out + extra_out).astype(jnp.bfloat16)
    rounded_in, rounded_out = lax.optimization_barrier((rounded_in, rounded_out))
    dp_count = lax.axis_size("dp")
    pieces_in = rounded_in.reshape(dp_count, width_model // dp_count, hidden_width)
    pieces_out = rounded_out.reshape(dp_count, hidden_width // dp_count, width_model)
    got_in, got_out = (
        lax.all_to_all(pieces_in, "dp", split_axis=0, concat_axis=0, tiled=True),
        lax.all_to_all(pieces_out, "dp", split_axis=0, concat_axis=0, tiled=True),
    )
    sum_in = jnp.sum(got_in, axis=0, dtype=jnp.float32)
    sum_out = jnp.sum(got_out, axis=0, dtype=jnp.float32)
    return (sum_in[None], sum_out[None])


def solution(mesh):
    in_specs = (
        P(("dp", "expert"), None),
        P(("dp", "expert"), None),
        P(("dp", "expert"), None),
        P(("dp", "expert"), None),
        P("expert", None, None),
        P("expert", None, None),
    )
    out_specs = (P("expert", "dp", None), P("expert", "dp", None))
    return jax.shard_map(body, mesh=mesh, in_specs=in_specs, out_specs=out_specs, check_vma=False)
```

profile of v0, /device:TPU:8, one launch (start us, length us, event | category | flops | bytes accessed | tf_op | source)
XLA Modules:
  0.0 554.2 jit_solution(3805775485658377749)
XLA Ops:
  0.6 0.8 copy.8
  1.4 0.1 reshape.139
  1.6 0.1 eq.31
  1.7 0.1 eq.27
  1.9 1.7 reduce-window.6
  3.6 0.3 slice_reduce_fusion
  3.9 0.1 fusion.13
  4.0 3.4 scatter_custom_fusion
  7.4 0.8 copy.12
  8.2 0.1 reshape.142
  8.4 0.0 copy-start.2
  8.4 2.8 gather_fusion.2
  11.2 0.1 mul.52
  11.3 4.3 gather_fusion.1
  15.7 4.3 fusion
  20.0 6.3 %all-to-all-start.1 = ((bf16[16,40,2560]{2,1,0:T(8,128)(2,1)}), bf16[16,40,2560]{2,1,0:T(8,128)(2,1)}, u32[]{:S(2)}, u32[]{:S(2)}) async-start(bf16[16,40,2560]{2,1,0:T(8,128)(2,1)} %fusion), calls=%async_computation.1 | async-start | bytes 6553600 | tf_op jit(solution)/shard_map/all_to_all | solution.py:74
  26.4 4.3 gather_fusion
  30.7 39.7 %all-to-all-done.1 = bf16[16,40,2560]{2,1,0:T(8,128)(2,1)} async-done(((bf16[16,40,2560]{2,1,0:T(8,128)(2,1)}), bf16[16,40,2560]{2,1,0:T(8,128)(2,1)}, u32[]{:S(2)}, u32[]{:S(2)}) %all-to-all-start.1) | async-done | bytes 3276832 | tf_op jit(solution)/shard_map/all_to_all | solution.py:74
  70.4 5.7 %all-to-all-start = ((bf16[16,40,2560]{2,1,0:T(8,128)(2,1)}), bf16[16,40,2560]{2,1,0:T(8,128)(2,1)S(1)}, u32[]{:S(2)}, u32[]{:S(2)}) async-start(bf16[16,40,2560]{2,1,0:T(8,128)(2,1)} %bitcast.53), calls=%async_computation | async-start | bytes 6553600 | tf_op jit(solution)/shard_map/all_to_all | solution.py:73
  76.0 3.4 collective-permute-start.2
  79.5 0.2 collective-permute-start.1
  79.7 2.5 slice.34
  82.2 3.3 collective-permute-start.5
  85.5 34.6 %all-to-all-done = bf16[16,40,2560]{2,1,0:T(8,128)(2,1)S(1)} async-done(((bf16[16,40,2560]{2,1,0:T(8,128)(2,1)}), bf16[16,40,2560]{2,1,0:T(8,128)(2,1)S(1)}, u32[]{:S(2)}, u32[]{:S(2)}) %all-to-all-start) | async-done | bytes 3276832 | tf_op jit(solution)/shard_map/all_to_all | solution.py:73
  120.2 1.2 slice.33
  121.4 2.4 collective-permute-start
  123.8 3.0 slice.32
  126.8 0.1 slice.31
  126.9 2.7 copy-done.4
  129.6 1.7 fusion.20
  131.3 9.7 %fusion.3 = f32[2560,768]{1,0:T(8,128)} fusion(bf16[384,2560]{1,0:T(8,128)(2,1)} %bitcast.60, bf16[384,2560]{1,0:T(8,128)(2,1)S(1)} %bitcast.57, f32[384,768]{1,0:T(8,128)S(1)} %fusion.20, bf16[1,768,2560]{2,1,0:T(8,128)(2,1)} %param.11), kind=kOutput, calls=%fused_computation.14 | convolution fusion | flops 3022553088 | bytes 16908288 | tf_op jit(solution)/shard_map/dot_general | solution.py:33
  141.0 59.7 %collective-permute-done.2 = bf16[2560,768]{1,0:T(8,128)(2,1)} collective-permute-done((bf16[2560,768]{1,0:T(8,128)(2,1)}, bf16[2560,768]{1,0:T(8,128)(2,1)}, u32[]{:S(2)}, u32[]{:S(2)}) %collective-permute-start.2) | collective-permute-done | bytes 3932192 | tf_op jit(solution)/shard_map/ppermute | solution.py:9
  200.7 3.8 multiply_convert_fusion.1
  204.5 80.5 %collective-permute-done.1 = bf16[768,2560]{1,0:T(8,128)(2,1)} collective-permute-done((bf16[768,2560]{1,0:T(8,128)(2,1)}, bf16[768,2560]{1,0:T(8,128)(2,1)}, u32[]{:S(2)}, u32[]{:S(2)}) %collective-permute-start.1) | collective-permute-done | bytes 3932192 | tf_op jit(solution)/shard_map/ppermute | solution.py:9
  285.0 3.9 fusion.2
  288.9 0.0 slice-start.1
  288.9 0.1 collective-permute-start.3
  289.0 2.3 fusion.8
  291.3 3.8 collective-permute-start.4
  295.1 54.3 %collective-permute-done.3 = bf16[256,768]{1,0:T(8,128)(2,1)S(1)} collective-permute-done((bf16[256,768]{1,0:T(8,128)(2,1)S(1)}, bf16[256,768]{1,0:T(8,128)(2,1)S(1)}, u32[]{:S(2)}, u32[]{:S(2)}) %collective-permute-start.3) | collective-permute-done | bytes 393248 | tf_op jit(solution)/shard_map/ppermute | solution.py:9
  349.5 4.5 add_convert_fusion.1
  354.0 3.3 collective-permute-done.4
  357.3 2.6 add_convert_fusion
  359.9 98.0 %all_to_all.20 = bf16[16,48,2560]{2,1,0:T(8,128)(2,1)} all-to-all(bf16[16,48,2560]{2,1,0:T(8,128)(2,1)S(1)} %bitcast.52), channel_id=1, replica_groups=mesh['dp'=16,'expert'=16] {'dp'}, dimensions={0} | all-to-all | bytes 7864320 | tf_op jit(solution)/shard_map/all_to_all | solution.py:99
  457.9 4.9 all-to-all-start.2
  462.8 3.5 convert_reduce_fusion
  466.3 84.5 %all-to-all-done.2 = bf16[16,160,768]{2,1,0:T(8,128)(2,1)} async-done(((bf16[16,160,768]{2,1,0:T(8,128)(2,1)}), bf16[16,160,768]{2,1,0:T(8,128)(2,1)}, u32[]{:S(2)}, u32[]{:S(2)}) %all-to-all-start.2) | async-done | bytes 3932192 | tf_op jit(solution)/shard_map/all_to_all | solution.py:98
  550.8 3.5 convert_reduce_fusion.1
  (23 shorter events, 0.2 us)
Async XLA Ops:
  8.4 2.9 copy-start.2
  20.0 6.3 %copy-start.3 = (bf16[128,2560]{1,0:T(8,128)(2,1)S(1)}, bf16[128,2560]{1,0:T(8,128)(2,1)}, u32[]{:S(2)}) copy-start(bf16[128,2560]{1,0:T(8,128)(2,1)} %param.6) | copy-start | bytes 1966084
  20.0 50.4 %all-to-all-start.1 = ((bf16[16,40,2560]{2,1,0:T(8,128)(2,1)}), bf16[16,40,2560]{2,1,0:T(8,128)(2,1)}, u32[]{:S(2)}, u32[]{:S(2)}) async-start(bf16[16,40,2560]{2,1,0:T(8,128)(2,1)} %fusion), calls=%async_computation.1 | async-start | bytes 6553600 | tf_op jit(solution)/shard_map/all_to_all | solution.py:74
  70.4 49.8 %all-to-all-start = ((bf16[16,40,2560]{2,1,0:T(8,128)(2,1)}), bf16[16,40,2560]{2,1,0:T(8,128)(2,1)S(1)}, u32[]{:S(2)}, u32[]{:S(2)}) async-start(bf16[16,40,2560]{2,1,0:T(8,128)(2,1)} %bitcast.53), calls=%async_computation | async-start | bytes 6553600 | tf_op jit(solution)/shard_map/all_to_all | solution.py:73
  76.0 124.7 %collective-permute-start.2 = (bf16[2560,768]{1,0:T(8,128)(2,1)}, bf16[2560,768]{1,0:T(8,128)(2,1)}, u32[]{:S(2)}, u32[]{:S(2)}) collective-permute-start(bf16[2560,768]{1,0:T(8,128)(2,1)} %bitcast.64), channel_id=1, source_target_pairs={{0,8},{1,9},{2,10},{3,11},{4,12},{5,13},{6,14},{7,15},{8,0},{9,1},... | collective-permute-start | bytes 11796488 | tf_op jit(solution)/shard_map/ppermute | solution.py:9
  79.5 205.5 %collective-permute-start.1 = (bf16[768,2560]{1,0:T(8,128)(2,1)}, bf16[768,2560]{1,0:T(8,128)(2,1)}, u32[]{:S(2)}, u32[]{:S(2)}) collective-permute-start(bf16[768,2560]{1,0:T(8,128)(2,1)} %bitcast.65), channel_id=1, source_target_pairs={{0,8},{1,9},{2,10},{3,11},{4,12},{5,13},{6,14},{7,15},{8,0},{9,1},... | collective-permute-start | bytes 11796488 | tf_op jit(solution)/shard_map/ppermute | solution.py:9
  82.2 275.2 %collective-permute-start.5 = (bf16[256,2560]{1,0:T(8,128)(2,1)}, bf16[256,2560]{1,0:T(8,128)(2,1)}, u32[]{:S(2)}, u32[]{:S(2)}) collective-permute-start(bf16[256,2560]{1,0:T(8,128)(2,1)} %bitcast.8), channel_id=1, source_target_pairs={{0,8},{1,9},{2,10},{3,11},{4,12},{5,13},{6,14},{7,15},{8,0},{9,1},... | collective-permute-start | bytes 3932168 | tf_op jit(solution)/shard_map/ppermute | solution.py:9
  121.4 228.1 %collective-permute-start = (bf16[256,2560]{1,0:T(8,128)(2,1)}, bf16[256,2560]{1,0:T(8,128)(2,1)}, u32[]{:S(2)}, u32[]{:S(2)}) collective-permute-start(bf16[256,2560]{1,0:T(8,128)(2,1)} %bitcast.7), channel_id=1, source_target_pairs={{0,8},{1,9},{2,10},{3,11},{4,12},{5,13},{6,14},{7,15},{8,0},{9,1},... | collective-permute-start | bytes 3932168 | tf_op jit(solution)/shard_map/ppermute | solution.py:9
  126.8 2.8 copy-start.4
  126.9 4.4 copy-start.1
  129.6 1.7 copy-start
  285.0 64.5 %slice-start = ((s8[7864320]{0:T(1024)(128)(4,1)}), s8[4194304]{0:T(1024)(128)(4,1)S(1)}, s32[]{:S(2)}) async-start(s8[7864320]{0:T(1024)(128)(4,1)} %bitcast.55), calls=%async_computation.4 | async-start | bytes 8388608
  288.9 60.6 %slice-start.1 = ((s8[7864320]{0:T(1024)(128)(4,1)}), s8[3670016]{0:T(1024)(128)(4,1)S(1)}, s32[]{:S(2)}) async-start(s8[7864320]{0:T(1024)(128)(4,1)} %bitcast.55), calls=%async_computation.5 | async-start | bytes 7340032
  288.9 60.6 %collective-permute-start.3 = (bf16[256,768]{1,0:T(8,128)(2,1)S(1)}, bf16[256,768]{1,0:T(8,128)(2,1)S(1)}, u32[]{:S(2)}, u32[]{:S(2)}) collective-permute-start(bf16[256,768]{1,0:T(8,128)(2,1)S(1)} %fusion.2), channel_id=1, source_target_pairs={{0,8},{1,9},{2,10},{3,11},{4,12},{5,13},{6,14},{7,15},{8,0},{9,1},... | collective-permute-start | bytes 1179656 | tf_op jit(solution)/shard_map/ppermute | solution.py:9
  291.3 66.0 %collective-permute-start.4 = (bf16[256,768]{1,0:T(8,128)(2,1)S(1)}, bf16[256,768]{1,0:T(8,128)(2,1)S(1)}, u32[]{:S(2)}, u32[]{:S(2)}) collective-permute-start(bf16[256,768]{1,0:T(8,128)(2,1)S(1)} %get-tuple-element.8), channel_id=1, source_target_pairs={{0,8},{1,9},{2,10},{3,11},{4,12},{5,13},{6,14},{7,15},{8,0},{9,1},... | collective-permute-start | bytes 1179656 | tf_op jit(solution)/shard_map/ppermute | solution.py:9
  457.9 92.8 %all-to-all-start.2 = ((bf16[16,160,768]{2,1,0:T(8,128)(2,1)}), bf16[16,160,768]{2,1,0:T(8,128)(2,1)}, u32[]{:S(2)}, u32[]{:S(2)}) async-start(bf16[16,160,768]{2,1,0:T(8,128)(2,1)} %bitcast.51), calls=%async_computation.2 | async-start | bytes 7864320 | tf_op jit(solution)/shard_map/all_to_all | solution.py:98
where the time goes:
time: 556 us; the launch traced here: 554 us
  waiting for transfers between devices  357 us (64%)
  blocking collectives  98 us (18%)
  starting transfers between devices  30.1 us (5%)
  matrix products  28.5 us (5%)
  local copies, waits for them, and re-layouts  27 us (5%)
  other arithmetic  13.2 us (2%)
    ppermute x6, waiting for transfers between devices, shifted(): lax.ppermute(x, axis, [(i, (i + by) % devices) for i in range(devices)])  198 us
    all_to_all x1, blocking collectives, body(): lax.all_to_all(pieces_out, 'dp', split_axis=0, concat_axis=0, tiled=True)  98 us
    all_to_all x1, waiting for transfers between devices, body(): lax.all_to_all(pieces_in, 'dp', split_axis=0, concat_axis=0, tiled=True)  84.5 us
    all_to_all x1, waiting for transfers between devices, body(): lax.all_to_all(sent_grads, 'expert', split_axis=0, concat_axis=0, tiled=T...  39.7 us
    all_to_all x1, waiting for transfers between devices, body(): lax.all_to_all(sent_inputs, 'expert', split_axis=0, concat_axis=0, tiled=...  34.6 us
    dot_general x2, matrix products, outer_sums(): lax.dot_general(rows_in, pre_grad, (((0,), (0,)), ((), ())), preferred_el...  14.2 us
    ppermute x6, starting transfers between devices, shifted(): lax.ppermute(x, axis, [(i, (i + by) % devices) for i in range(devices)])  13.3 us
  transfers between devices with their start and end apart: 9, of which 7 were waited for; matrix products, arithmetic and copies ran while one was open for 7% of the time, Pallas kernels for 0%

commit v1 on v0

v1 whole, which is shorter than its diff:
```python
import jax
import jax.numpy as jnp
from jax import lax
from jax.sharding import PartitionSpec as P


def silu_slope(values):
    sigma = jax.nn.sigmoid(values)
    return sigma * (1.0 + values * (1.0 - sigma))


def forward_rows(rows_in, weight_in):
    pre_act = jnp.dot(rows_in, weight_in, preferred_element_type=jnp.float32)
    return (pre_act, jax.nn.silu(pre_act).astype(jnp.bfloat16))


def backward_rows(rows_grad, weight_out, pre_act):
    back_grad = lax.dot_general(
        rows_grad, weight_out, (((1,), (1,)), ((), ())), preferred_element_type=jnp.float32
    )
    return (back_grad * silu_slope(pre_act)).astype(jnp.bfloat16)


def outer_sums(rows_in, rows_grad, hidden, pre_grad):
    grad_o = lax.dot_general(
        hidden, rows_grad, (((0,), (0,)), ((), ())), preferred_element_type=jnp.float32
    )
    grad_i = lax.dot_general(
        rows_in, pre_grad, (((0,), (0,)), ((), ())), preferred_element_type=jnp.float32
    )
    return (grad_i, grad_o)


def body(tokens, routing, gates, cotangent, w_in, w_out):
    peer_count = lax.axis_size("expert")
    tok_count = tokens.shape[0]
    top_count = routing.shape[1]
    width_model = tokens.shape[1]
    hidden_width = w_in.shape[2]
    entries = tok_count * top_count
    capacity = tok_count * top_count * 5 // (peer_count * 6)
    chosen = routing.reshape(entries)
    onehot = (chosen[:, None] == jnp.arange(peer_count, dtype=jnp.int32)[None, :]).astype(jnp.int32)
    earlier = jnp.cumsum(onehot, axis=0) - onehot
    rank_of = jnp.sum(earlier * onehot, axis=1)
    target = jnp.where(rank_of < capacity, chosen * capacity + rank_of, peer_count * capacity)
    slot_entry = jnp.full((peer_count * capacity,), entries, jnp.int32)
    slot_entry = slot_entry.at[target].set(jnp.arange(entries, dtype=jnp.int32), mode="drop")
    token_of = slot_entry // top_count
    padded_tokens = jnp.concatenate([tokens, jnp.zeros((1, width_model), tokens.dtype)], axis=0)
    padded_cots = jnp.concatenate([cotangent, jnp.zeros((1, width_model), cotangent.dtype)], axis=0)
    padded_gates = jnp.concatenate([gates.reshape(entries), jnp.zeros((1,), jnp.float32)], axis=0)
    sent_inputs = padded_tokens[token_of].reshape(peer_count, capacity, width_model)
    sent_grads = (
        padded_cots[token_of].astype(jnp.float32) * padded_gates[slot_entry][:, None]
    ).astype(jnp.bfloat16)
    sent_grads = sent_grads.reshape(peer_count, capacity, width_model)
    weight_in = w_in[0]
    weight_out = w_out[0]
    got_inputs, got_grads = (
        lax.all_to_all(sent_inputs, "expert", split_axis=0, concat_axis=0, tiled=True),
        lax.all_to_all(sent_grads, "expert", split_axis=0, concat_axis=0, tiled=True),
    )
    rows_in = got_inputs.reshape(peer_count * capacity, width_model)
    rows_grad = got_grads.reshape(peer_count * capacity, width_model)
    pre_act, hidden = forward_rows(rows_in, weight_in)
    pre_grad = backward_rows(rows_grad, weight_out, pre_act)
    part_in, part_out = outer_sums(rows_in, rows_grad, hidden, pre_grad)
    rounded_in = part_in.astype(jnp.bfloat16)
    rounded_out = part_out.astype(jnp.bfloat16)
    sum_in = lax.psum_scatter(rounded_in, "dp", scatter_dimension=0, tiled=True).astype(jnp.float32)
    sum_out = lax.psum_scatter(rounded_out, "dp", scatter_dimension=0, tiled=True).astype(jnp.float32)
    return (sum_in[None], sum_out[None])


def solution(mesh):
    in_specs = (
        P(("dp", "expert"), None),
        P(("dp", "expert"), None),
        P(("dp", "expert"), None),
        P(("dp", "expert"), None),
        P("expert", None, None),
        P("expert", None, None),
    )
    out_specs = (P("expert", "dp", None), P("expert", "dp", None))
    return jax.shard_map(body, mesh=mesh, in_specs=in_specs, out_specs=out_specs, check_vma=False)
```

time: 556 us -> 299 us (0.54)
  waiting for transfers between devices: 357 us -> 216 us
  blocking collectives: 98 us -> 0 us
  starting transfers between devices: 30.1 us -> 12.2 us
  between operations: 0.88 us -> 14.2 us
  local copies, waits for them, and re-layouts: 27 us -> 17.9 us
    ppermute x6 -> x0, waiting for transfers between devices: 198 us -> none  [shifted(): lax.ppermute(x, axis, [(i, (i + by) % devices) for i in range(devices)])]
    reduce_scatter x0 -> x2, waiting for transfers between devices: none -> 147 us  [the longest x1 77.9 us: body(): lax.psum_scatter(rounded_in, 'dp', scatter_dimension=0, tiled=True)]
    all_to_all x1 -> x0, blocking collectives: 98 us -> none  [body(): lax.all_to_all(pieces_out, 'dp', split_axis=0, concat_axis=0, tiled=True)]
    all_to_all x1 -> x0, waiting for transfers between devices: 84.5 us -> none  [body(): lax.all_to_all(pieces_in, 'dp', split_axis=0, concat_axis=0, tiled=True)]
    ppermute x6 -> x0, starting transfers between devices: 13.3 us -> none  [shifted(): lax.ppermute(x, axis, [(i, (i + by) % devices) for i in range(devices)])]
    dot_general x2 -> x1, matrix products: 14.2 us -> 7.2 us  [outer_sums(): lax.dot_general(rows_in, pre_grad, (((0,), (0,)), ((), ())), preferred_el...]
    reduce_sum x2 -> x0, other arithmetic: 6.95 us -> none  [the longest x1 3.48 us: body(): sum_out = jnp.sum(got_out, axis=0, dtype=jnp.float32)]
    slice x5 -> x1, local copies, waits for them, and re-layouts: 7.11 us -> 0.25 us  [the longest x1 2.99 us: body(): rows_grad = got_grads[:, :own_slots, :].reshape(own_count, width_model)]
  transfers between devices with their start and end apart: 9 -> 4, of which waited for: 7 -> 4; matrix products, arithmetic and copies ran while one was open for 7% -> 11% of each run, Pallas kernels for 0% -> 0%
where the time goes in v1:
time: 299 us; the launch traced here: 298 us
  waiting for transfers between devices  216 us (72%)
  matrix products  26.4 us (9%)
  local copies, waits for them, and re-layouts  17.9 us (6%)
  between operations  14.2 us (5%)
  starting transfers between devices  12.2 us (4%)
  other arithmetic  10.4 us (3%)
    reduce_scatter x1, waiting for transfers between devices, body(): lax.psum_scatter(rounded_in, 'dp', scatter_dimension=0, tiled=True)  77.9 us
    reduce_scatter x1, waiting for transfers between devices, body(): lax.psum_scatter(rounded_out, 'dp', scatter_dimension=0, tiled=True)  69.2 us
    all_to_all x1, waiting for transfers between devices, body(): lax.all_to_all(sent_grads, 'expert', split_axis=0, concat_axis=0, tiled=T...  37 us
    all_to_all x1, waiting for transfers between devices, body(): lax.all_to_all(sent_inputs, 'expert', split_axis=0, concat_axis=0, tiled=...  32.2 us
    dot_general x1, matrix products, outer_sums(): lax.dot_general(rows_in, pre_grad, (((0,), (0,)), ((), ())), preferred_el...  7.2 us
    dot_general x1, matrix products, forward_rows(): pre_act = jnp.dot(rows_in, weight_in, preferred_element_type=jnp.float32)  7.09 us
    dot_general x1, matrix products, outer_sums(): lax.dot_general(hidden, rows_grad, (((0,), (0,)), ((), ())), preferred_el...  6.44 us
    all_to_all x1, starting transfers between devices, body(): lax.all_to_all(sent_inputs, 'expert', split_axis=0, concat_axis=0, tiled=...  6.31 us
  transfers between devices with their start and end apart: 4, of which 4 were waited for; matrix products, arithmetic and copies ran while one was open for 11% of the time, Pallas kernels for 0%

profile of v1, /device:TPU:8, one launch (start us, length us, event | category | flops | bytes accessed | tf_op | source)
XLA Modules:
  0.0 297.5 jit_solution(8121117989963715208)
XLA Ops:
  7.2 0.7 broadcast_multiply_fusion
  7.9 0.8 copy.8
  8.6 0.1 eq.29
  8.8 0.1 eq.25
  8.9 0.1 copy.11
  9.0 0.1 mul.42
  9.2 1.7 reduce-window.6
  10.9 0.3 slice_reduce_fusion
  11.2 0.1 fusion.10
  11.3 3.4 %scatter_custom_fusion = s32[640]{0:T(1024)S(1)} fusion(s32[768]{0:T(1024)S(1)} %fusion.13, s32[768]{0:T(1024)S(1)} %iota.11, s32[]{:T(128)} %constant.13.clone.1), kind=kCustom, calls=%fused_computation.40 | custom fusion | bytes 2564 | tf_op jit(solution)/shard_map/scatter | solution.py:48
  14.8 1.1 concatenate.9
  15.9 4.3 %gather_fusion = bf16[640,2560]{1,0:T(8,128)(2,1)} fusion(bf16[129,2560]{1,0:T(8,128)(2,1)S(1)} %concatenate.9, s32[1024]{0:T(1024)S(1)} %get-tuple-element.5), kind=kCustom, calls=%fused_computation | custom fusion | bytes 6556160 | tf_op jit(solution)/shard_map/gather | solution.py:53
  20.2 0.0 copy-start.1
  20.2 6.3 %all-to-all-start = ((bf16[16,40,2560]{2,1,0:T(8,128)(2,1)}), bf16[16,40,2560]{2,1,0:T(8,128)(2,1)}, u32[]{:S(2)}, u32[]{:S(2)}) async-start(bf16[16,40,2560]{2,1,0:T(8,128)(2,1)} %bitcast.45), calls=%async_computation | async-start | bytes 6553600 | tf_op jit(solution)/shard_map/all_to_all | solution.py:61
  26.5 0.0 copy-done.1
  26.5 0.0 copy-start
  26.6 0.1 copy.12
  26.7 0.1 reshape.81
  26.8 2.8 gather_fusion.2
  29.6 0.1 mul.43
  29.7 0.0 copy-done
  29.8 4.4 %gather_fusion.1 = bf16[640,2560]{1,0:T(8,128)(2,1)} fusion(bf16[129,2560]{1,0:T(8,128)(2,1)S(1)} %concatenate.10, s32[1024]{0:T(1024)S(1)} %get-tuple-element.5), kind=kCustom, calls=%fused_computation.1 | custom fusion | bytes 6556160 | tf_op jit(solution)/shard_map/gather | solution.py:55
  34.1 4.3 %fusion = bf16[16,40,2560]{2,1,0:T(8,128)(2,1)} fusion(bf16[16,40,2560]{2,1,0:T(8,128)(2,1)} %bitcast.46, f32[16,40]{1,0:T(8,128)S(1)} %mul.43), kind=kLoop, calls=%fused_computation.5 | loop fusion | flops 4915200 | bytes 6556160 | tf_op jit(solution)/shard_map/convert_element_type | solution.py:56
  38.4 32.2 %all-to-all-done = bf16[16,40,2560]{2,1,0:T(8,128)(2,1)} async-done(((bf16[16,40,2560]{2,1,0:T(8,128)(2,1)}), bf16[16,40,2560]{2,1,0:T(8,128)(2,1)}, u32[]{:S(2)}, u32[]{:S(2)}) %all-to-all-start) | async-done | bytes 3276832 | tf_op jit(solution)/shard_map/all_to_all | solution.py:61
  70.6 5.7 %all-to-all-start.1 = ((bf16[16,40,2560]{2,1,0:T(8,128)(2,1)}), bf16[16,40,2560]{2,1,0:T(8,128)(2,1)S(1)}, u32[]{:S(2)}, u32[]{:S(2)}) async-start(bf16[16,40,2560]{2,1,0:T(8,128)(2,1)} %fusion), calls=%async_computation.1 | async-start | bytes 6553600 | tf_op jit(solution)/shard_map/all_to_all | solution.py:62
  76.3 0.0 reduce-scatter.5.cloned.1.call-start
  76.3 7.1 %fusion.1 = f32[640,768]{1,0:T(8,128)} fusion(bf16[640,2560]{1,0:T(8,128)(2,1)} %bitcast.2, bf16[1,2560,768]{2,1,0:T(8,128)(2,1)} %param.10), kind=kOutput, calls=%fused_computation.8 | convolution fusion | flops 2516582400 | bytes 9175040 | tf_op jit(solution)/shard_map/dot_general | solution.py:13
  83.4 37.0 %all-to-all-done.1 = bf16[16,40,2560]{2,1,0:T(8,128)(2,1)S(1)} async-done(((bf16[16,40,2560]{2,1,0:T(8,128)(2,1)}), bf16[16,40,2560]{2,1,0:T(8,128)(2,1)S(1)}, u32[]{:S(2)}, u32[]{:S(2)}) %all-to-all-start.1) | async-done | bytes 3276832 | tf_op jit(solution)/shard_map/all_to_all | solution.py:62
  120.4 6.4 %convolution_convert_fusion = bf16[768,2560]{1,0:T(8,128)(2,1)} fusion(bf16[640,2560]{1,0:T(8,128)(2,1)S(1)} %bitcast.47, f32[640,768]{1,0:T(8,128)} %fusion.1), kind=kOutput, calls=%fused_computation.6 | convolution fusion | flops 2521006080 | bytes 9175040 | tf_op jit(solution)/shard_map/dot_general | solution.py:25
  126.9 0.0 reduce-scatter.5.cloned.1.call-update
  126.9 0.2 reduce-scatter.3.cloned.1.call-start
  127.1 5.7 %multiply_convert_fusion.1 = bf16[640,768]{1,0:T(8,128)(2,1)S(1)} fusion(f32[640,768]{1,0:T(8,128)} %fusion.1, bf16[640,2560]{1,0:T(8,128)(2,1)S(1)} %bitcast.48, bf16[1,768,2560]{2,1,0:T(8,128)(2,1)} %param.11), kind=kOutput, calls=%fused_computation.13 | convolution fusion | flops 2521006080 | bytes 10158080 | tf_op jit(solution)/shard_map/dot_general | solution.py:18
  132.8 7.2 %convolution_convert_fusion.1 = bf16[2560,768]{1,0:T(8,128)(2,1)} fusion(bf16[640,2560]{1,0:T(8,128)(2,1)} %bitcast.2, bf16[640,768]{1,0:T(8,128)(2,1)S(1)} %multiply_convert_fusion.1), kind=kOutput, calls=%fused_computation.7 | convolution fusion | flops 2518548480 | bytes 8192000 | tf_op jit(solution)/shard_map/dot_general | solution.py:28
  140.0 0.0 reduce-scatter.3.cloned.1.call-update
  140.1 69.2 %reduce-scatter.5.cloned.1.call-done = bf16[48,2560]{1,0:T(8,128)(2,1)} async-done(((bf16[768,2560]{1,0:T(8,128)(2,1)}), bf16[48,2560]{1,0:T(8,128)(2,1)}) %reduce-scatter.5.cloned.1.call-update) | async-done | bytes 245776 | tf_op jit(solution)/shard_map/reduce_scatter | solution.py:72
  209.3 1.8 bitcast_convert_fusion
  211.0 77.9 %reduce-scatter.3.cloned.1.call-done = bf16[160,768]{1,0:T(8,128)(2,1)} async-done(((bf16[2560,768]{1,0:T(8,128)(2,1)}), bf16[160,768]{1,0:T(8,128)(2,1)}) %reduce-scatter.3.cloned.1.call-update) | async-done | bytes 245776 | tf_op jit(solution)/shard_map/reduce_scatter | solution.py:71
  289.0 1.8 bitcast_convert_fusion.1
  (8 shorter events, 0.1 us)
Async XLA Ops:
  20.2 6.3 %copy-start.1 = (f32[128,6]{0,1:T(8,128)S(1)}, f32[128,6]{0,1:T(8,128)}, u32[]{:S(2)}) copy-start(f32[128,6]{0,1:T(8,128)} %param.8) | copy-start | bytes 9220
  20.2 50.4 %all-to-all-start = ((bf16[16,40,2560]{2,1,0:T(8,128)(2,1)}), bf16[16,40,2560]{2,1,0:T(8,128)(2,1)}, u32[]{:S(2)}, u32[]{:S(2)}) async-start(bf16[16,40,2560]{2,1,0:T(8,128)(2,1)} %bitcast.45), calls=%async_computation | async-start | bytes 6553600 | tf_op jit(solution)/shard_map/all_to_all | solution.py:61
  26.5 3.2 %copy-start = (bf16[128,2560]{1,0:T(8,128)(2,1)S(1)}, bf16[128,2560]{1,0:T(8,128)(2,1)}, u32[]{:S(2)}) copy-start(bf16[128,2560]{1,0:T(8,128)(2,1)} %param.9) | copy-start | bytes 1966084
  70.6 49.8 %all-to-all-start.1 = ((bf16[16,40,2560]{2,1,0:T(8,128)(2,1)}), bf16[16,40,2560]{2,1,0:T(8,128)(2,1)S(1)}, u32[]{:S(2)}, u32[]{:S(2)}) async-start(bf16[16,40,2560]{2,1,0:T(8,128)(2,1)} %fusion), calls=%async_computation.1 | async-start | bytes 6553600 | tf_op jit(solution)/shard_map/all_to_all | solution.py:62
  76.3 133.0 %reduce-scatter.5.cloned.1.call-start = ((), (), s32[]{:S(2)}) async-start(), calls=%async_computation.5 | async-start | bytes 4177920 | tf_op jit(solution)/shard_map/reduce_scatter | solution.py:72
  126.9 162.1 %reduce-scatter.3.cloned.1.call-start = ((), (), s32[]{:S(2)}) async-start(), calls=%async_computation.4 | async-start | bytes 4177920 | tf_op jit(solution)/shard_map/reduce_scatter | solution.py:71
Sparse Core Ops, SparseCore 0:
  127.0 82.2 reduce-scatter.4
  211.9 77.0 reduce-scatter.2

commit v2 on v1

v2 whole, which is shorter than its diff:
```python
import functools

import jax
import jax.numpy as jnp
from jax import lax
from jax.experimental import pallas as pl
from jax.experimental.pallas import tpu as pltpu
from jax.sharding import PartitionSpec as P

MESH = pl.DeviceIdType.MESH
BF = jnp.bfloat16
F32 = jnp.float32
NEX = 16
CAP = 40
ROWS = NEX * CAP
TOK_SPLIT = 2
COT_SPLIT = 4
IN_UNITS = 3
RING = 8
HOPS = [(0, 1, 0)] + [(0, s, p) for s in (2, 3, 4) for p in (0, 1)]
HOPS += [(1, 1, 1)] + [(1, s, p) for s in (2, 3, 4) for p in (0, 1)]
HOP = {hop: i for i, hop in enumerate(HOPS)}


def silu_slope(values):
    sigma = jax.nn.sigmoid(values)
    return sigma * (1.0 + values * (1.0 - sigma))


def mm(a, b, dims):
    return lax.dot_general(a, b, (dims, ((), ())), preferred_element_type=F32)


def kernel(routing, gates, tok, cot, win_hbm, wout_hbm, gin, gout,
           win, wout, stok, scot, rtok, rcot, tokf, cotb, onehot, pre, slope, back, hid, pgrad,
           po, pi, rzo, rzi, yso, yro, ysi, yri,
           wsem, lsem, ts, tr, cs, cr, zos, zor, zis, zir, yos, yor, yis, yir):
    me = lax.axis_index("expert")
    dp = lax.axis_index("dp")
    yl = dp // RING
    z = lax.rem(dp, RING)
    up = {"dp": yl * RING + lax.rem(z + 1, RING)}
    down = {"dp": yl * RING + lax.rem(z + RING - 1, RING)}
    side = {"dp": (1 - yl) * RING + z}
    width = tok.shape[1]
    toks = tok.shape[0]

    copies = []
    for i, (src, dst) in enumerate(((win_hbm, win), (wout_hbm, wout))):
        copy = pltpu.make_async_copy(src.at[0], dst, wsem.at[i])
        copy.start()
        copies.append(copy)

    barrier = pltpu.get_barrier_semaphore()
    for o in range(1, NEX):
        pl.semaphore_signal(barrier, inc=1, device_id={"expert": lax.rem(me + o, NEX)}, device_id_type=MESH)
    for peer in (up, down, side):
        pl.semaphore_signal(barrier, inc=1, device_id=peer, device_id_type=MESH)

    expert = lax.broadcasted_iota(jnp.int32, (NEX, toks), 0)
    member = jnp.zeros((NEX, toks), F32)
    weight = jnp.zeros((NEX, toks), F32)
    for k in range(routing.shape[0]):
        hit = routing[k : k + 1, :] == expert
        member = jnp.where(hit, 1.0, member)
        weight = jnp.where(hit, gates[k : k + 1, :], weight)
    before = lax.broadcasted_iota(jnp.int32, (toks, toks), 0) < lax.broadcasted_iota(jnp.int32, (toks, toks), 1)
    rank = mm(member.astype(BF), jnp.where(before, 1.0, 0.0).astype(BF), ((1,), (0,)))
    rank = jnp.where(member > 0.0, rank, -1.0)
    place = lax.broadcasted_iota(jnp.int32, (NEX, CAP, toks), 1).astype(F32)
    match = place == rank[:, None, :]
    onehot[...] = jnp.where(match, 1.0, 0.0).reshape(ROWS, toks).astype(BF)
    gate = jnp.sum(jnp.where(match, weight[:, None, :], 0.0), axis=2, keepdims=True).reshape(ROWS, 1)

    pl.semaphore_wait(barrier, NEX + 2)

    def dispatch(source, send, recv, ssem, rsem, splits, which, scale):
        size = width // splits
        out = []
        for k in range(splits):
            step = 256 if size % 256 == 0 else 128
            for c in range(k * size, (k + 1) * size, step):
                value = mm(onehot[...], source[:, c : c + step], ((1,), (0,)))
                if scale is not None:
                    value = value * scale
                send[:, :, c : c + step] = value.reshape(NEX, CAP, step).astype(BF)
            span = pl.ds(k * size, size)
            row = []
            for o in range(1, NEX):
                target = lax.rem(me + o, NEX)
                copy = pltpu.make_async_remote_copy(
                    src_ref=send.at[target, :, span], dst_ref=recv.at[me, :, span],
                    send_sem=ssem.at[k, o - 1], recv_sem=rsem.at[k, o - 1],
                    device_id={"expert": target}, device_id_type=MESH)
                copy.start()
                row.append(copy)
            own = pltpu.make_async_copy(send.at[me, :, span], recv.at[me, :, span], lsem.at[which, k])
            own.start()
            out.append((row, own))
        return out

    tok_copies = dispatch(tok, stok, rtok, ts, tr, TOK_SPLIT, 0, None)
    cot_copies = dispatch(cot, scot, rcot, cs, cr, COT_SPLIT, 1, gate)

    def arrived(entry):
        row, own = entry
        own.wait()
        for copy in row:
            copy.wait_recv()

    def pieces(distance):
        d = lax.rem(z + distance + RING, RING)
        return ((1 - yl) * RING + d, yl * RING + d)

    def unit_copy(part, landing, ssem, rsem, u, direction, s, p):
        d = 5 - s if direction == 0 else s - 5
        hop = HOP[(direction, s, p)]
        return pltpu.make_async_remote_copy(
            src_ref=part.at[u, pieces(d)[p]], dst_ref=landing.at[u, hop],
            send_sem=ssem.at[u, hop], recv_sem=rsem.at[u, hop],
            device_id=up if direction == 0 else down, device_id_type=MESH)

    def ring_step(group, u, s):
        part, landing, ssem, rsem = group[:4]
        for p in (0, 1):
            for direction in (0, 1):
                if (direction, s, p) not in HOP:
                    continue
                if (direction, s - 1, p) in HOP:
                    unit_copy(part, landing, ssem, rsem, u, direction, s - 1, p).wait_recv()
                    index = pieces(5 - s if direction == 0 else s - 5)[p]
                    got = landing[u, HOP[(direction, s - 1, p)]].astype(F32)
                    part[u, index] = (part[u, index].astype(F32) + got).astype(BF)
                unit_copy(part, landing, ssem, rsem, u, direction, s, p).start()

    def side_copy(group, u):
        ysend, yrecv, yssem, yrsem = group[4:8]
        return pltpu.make_async_remote_copy(
            src_ref=ysend.at[u], dst_ref=yrecv.at[u], send_sem=yssem.at[u], recv_sem=yrsem.at[u],
            device_id=side, device_id_type=MESH)

    def ring_end(group, u):
        part, landing, ssem, rsem = group[:4]
        ysend, out, cols = group[4], group[8], group[9]
        for p in (0, 1):
            for direction in (0, 1):
                unit_copy(part, landing, ssem, rsem, u, direction, 4, p).wait_recv()
            total = part[u, pieces(0)[p]].astype(F32)
            total += landing[u, HOP[(0, 4, p)]].astype(F32) + landing[u, HOP[(1, 4, p)]].astype(F32)
            if p == 0:
                ysend[u] = total.astype(BF)
                side_copy(group, u).start()
            else:
                out[0, :, cols * u : cols * (u + 1)] = total

    def finish(group, u):
        part, landing, ssem, rsem = group[:4]
        yrecv, out, cols = group[5], group[8], group[9]
        side_copy(group, u).wait()
        out[0, :, cols * u : cols * (u + 1)] += yrecv[u].astype(F32)
        for direction, s, p in HOPS:
            unit_copy(part, landing, ssem, rsem, u, direction, s, p).wait_send()

    ff = win.shape[1]
    cblock = width // COT_SPLIT
    iblock = ff // IN_UNITS
    gro = (po, rzo, zos, zor, yso, yro, yos, yor, gout, cblock)
    gri = (pi, rzi, zis, zir, ysi, yri, yis, yir, gin, iblock)

    copies[0].wait()
    tblock = width // TOK_SPLIT
    for k in range(TOK_SPLIT):
        arrived(tok_copies[k])
        span = slice(k * tblock, (k + 1) * tblock)
        for j in range(0, NEX, 2):
            rows = rtok[j : j + 2, :, span].astype(F32).reshape(2 * CAP, tblock)
            tokf[j * CAP : (j + 2) * CAP, span] = rows.astype(BF)
        for n in range(0, ff, 256):
            value = mm(tokf[:, span], win[span, n : n + 256], ((1,), (0,)))
            if k > 0:
                value += pre[:, n : n + 256]
            if k < TOK_SPLIT - 1:
                pre[:, n : n + 256] = value
            else:
                hid[:, n : n + 256] = (value * jax.nn.sigmoid(value)).astype(BF)
                slope[:, n : n + 256] = silu_slope(value)

    copies[1].wait()
    for b in range(COT_SPLIT):
        arrived(cot_copies[b])
        span = slice(b * cblock, (b + 1) * cblock)
        for j in range(0, NEX, 2):
            rows = rcot[j : j + 2, :, span].astype(F32).reshape(2 * CAP, cblock)
            cotb[j * CAP : (j + 2) * CAP, :] = rows.astype(BF)
        for m in range(0, ff, 384):
            value = mm(hid[:, m : m + 384], cotb[...], ((0,), (0,)))
            po[b, m // 48 : (m + 384) // 48] = value.reshape(8, 48, cblock).astype(BF)
        ring_step(gro, b, 1)
        if b >= 1:
            ring_step(gro, b - 1, 3)
        for n in range(0, ff, 256):
            value = mm(cotb[...], wout[n : n + 256, span], ((1,), (1,)))
            if b > 0:
                value += back[:, n : n + 256]
            if b < COT_SPLIT - 1:
                back[:, n : n + 256] = value
            else:
                pgrad[:, n : n + 256] = (value * slope[:, n : n + 256]).astype(BF)
        ring_step(gro, b, 2)
        if b >= 1:
            ring_step(gro, b - 1, 4)
        if b >= 2:
            ring_end(gro, b - 2)

    last = COT_SPLIT - 1
    def part_in(u):
        for m in range(0, width, 640):
            value = mm(tokf[:, m : m + 640], pgrad[:, u * iblock : (u + 1) * iblock], ((0,), (0,)))
            pi[u, m // 160 : (m + 640) // 160] = value.reshape(4, 160, iblock).astype(BF)

    part_in(0)
    ring_step(gri, 0, 1)
    ring_step(gro, last, 3)
    ring_end(gro, last - 1)
    part_in(1)
    ring_step(gri, 1, 1)
    ring_step(gro, last, 4)
    part_in(2)
    ring_step(gri, 2, 1)
    for s in (2, 3, 4):
        for u in range(IN_UNITS):
            ring_step(gri, u, s)
        if s == 2:
            ring_end(gro, last)
    for u in range(IN_UNITS):
        ring_end(gri, u)
    for b in range(COT_SPLIT):
        finish(gro, b)
    for u in range(IN_UNITS):
        finish(gri, u)
    for row, _ in tok_copies + cot_copies:
        for copy in row:
            copy.wait_send()


def body(tokens, routing, gates, cotangent, w_in, w_out):
    width = tokens.shape[1]
    ff = w_in.shape[2]
    cblock = width // COT_SPLIT
    iblock = ff // IN_UNITS
    vmem = pl.BlockSpec(memory_space=pltpu.VMEM)
    hbm = pl.BlockSpec(memory_space=pl.ANY)
    dma = pltpu.SemaphoreType.DMA
    hops = len(HOPS)
    return pl.pallas_call(
        kernel,
        out_shape=(
            jax.ShapeDtypeStruct((1, width // 16, ff), F32),
            jax.ShapeDtypeStruct((1, ff // 16, width), F32),
        ),
        in_specs=[vmem, vmem, vmem, vmem, hbm, hbm],
        out_specs=(vmem, vmem),
        scratch_shapes=[
            pltpu.VMEM((width, ff), BF), pltpu.VMEM((ff, width), BF),
            pltpu.VMEM((NEX, CAP, width), BF), pltpu.VMEM((NEX, CAP, width), BF),
            pltpu.VMEM((NEX, CAP, width), BF), pltpu.VMEM((NEX, CAP, width), BF),
            pltpu.VMEM((ROWS, width), BF), pltpu.VMEM((ROWS, cblock), BF), pltpu.VMEM((ROWS, tokens.shape[0]), BF),
            pltpu.VMEM((ROWS, ff), F32), pltpu.VMEM((ROWS, ff), F32), pltpu.VMEM((ROWS, ff), F32),
            pltpu.VMEM((ROWS, ff), BF), pltpu.VMEM((ROWS, ff), BF),
            pltpu.VMEM((COT_SPLIT, 16, ff // 16, cblock), BF), pltpu.VMEM((IN_UNITS, 16, width // 16, iblock), BF),
            pltpu.VMEM((COT_SPLIT, hops, ff // 16, cblock), BF), pltpu.VMEM((IN_UNITS, hops, width // 16, iblock), BF),
            pltpu.VMEM((COT_SPLIT, ff // 16, cblock), BF), pltpu.VMEM((COT_SPLIT, ff // 16, cblock), BF),
            pltpu.VMEM((IN_UNITS, width // 16, iblock), BF), pltpu.VMEM((IN_UNITS, width // 16, iblock), BF),
            dma((2,)), dma((2, max(TOK_SPLIT, COT_SPLIT))),
            dma((TOK_SPLIT, NEX - 1)), dma((TOK_SPLIT, NEX - 1)),
            dma((COT_SPLIT, NEX - 1)), dma((COT_SPLIT, NEX - 1)),
            dma((COT_SPLIT, hops)), dma((COT_SPLIT, hops)),
            dma((IN_UNITS, hops)), dma((IN_UNITS, hops)),
            dma((COT_SPLIT,)), dma((COT_SPLIT,)), dma((IN_UNITS,)), dma((IN_UNITS,)),
        ],
        compiler_params=pltpu.CompilerParams(
            collective_id=0, has_side_effects=True, vmem_limit_bytes=62 * 1024 * 1024
        ),
    )(routing.T, gates.T, tokens, cotangent, w_in, w_out)


def solution(mesh):
    rows = P(("dp", "expert"), None)
    in_specs = (rows, rows, rows, rows, P("expert", None, None), P("expert", None, None))
    out_specs = (P("expert", "dp", None), P("expert", "dp", None))
    return jax.shard_map(body, mesh=mesh, in_specs=in_specs, out_specs=out_specs, check_vma=False)
```

time: 299 us -> 162 us (0.54)
  waiting for transfers between devices: 216 us -> 0 us
  Pallas kernels: 0 us -> 157 us
  matrix products: 26.4 us -> 0 us
  local copies, waits for them, and re-layouts: 17.9 us -> 3.68 us
  between operations: 14.2 us -> 0.64 us
  starting transfers between devices: 12.2 us -> 0 us
  other arithmetic: 10.4 us -> 0 us
    pallas_call x0 -> x1, Pallas kernels: none -> 157 us  [body(): pl.pallas_call(kernel, out_shape=(jax.ShapeDtypeStruct((1, width // 16, f...]
    reduce_scatter x2 -> x0, waiting for transfers between devices: 147 us -> none  [the longest x1 77.9 us: body(): lax.psum_scatter(rounded_in, 'dp', scatter_dimension=0, tiled=True)]
    all_to_all x2 -> x0, waiting for transfers between devices: 69.2 us -> none  [the longest x1 37 us: body(): lax.all_to_all(sent_grads, 'expert', split_axis=0, concat_axis=0, tiled=T...]
    dot_general x4 -> x0, matrix products: 26.4 us -> none  [the longest x1 7.2 us: outer_sums(): lax.dot_general(rows_in, pre_grad, (((0,), (0,)), ((), ())), preferred_el...]
    all_to_all x2 -> x0, starting transfers between devices: 12 us -> none  [the longest x1 6.31 us: body(): lax.all_to_all(sent_inputs, 'expert', split_axis=0, concat_axis=0, tiled=...]
    gather x3 -> x0, local copies, waits for them, and re-layouts: 11.5 us -> none  [the longest x1 4.36 us: body(): padded_cots[token_of].astype(jnp.float32)]
    convert_element_type x2 -> x0, other arithmetic: 4.28 us -> none  [the longest x1 4.27 us: body(): sent_grads = (padded_cots[token_of].astype(jnp.float32) * padded_gates[sl...]
    broadcast_in_dim x2 -> x0, other arithmetic: 3.51 us -> none  [body(): return (sum_in[None], sum_out[None])]
  transfers between devices with their start and end apart: 4 -> 0, of which waited for: 4 -> 0; matrix products, arithmetic and copies ran while one was open for 11% -> 0% of each run, Pallas kernels for 0% -> 0%
where the time goes in v2:
time: 162 us
  Pallas kernels  157 us (97%)
  local copies, waits for them, and re-layouts  3.68 us (2%)
    pallas_call x1, Pallas kernels, body(): pl.pallas_call(kernel, out_shape=(jax.ShapeDtypeStruct((1, width // 16, f...  157 us
    unnamed x2, local copies, waits for them, and re-layouts  3.68 us

profile of v2, /device:TPU:8, one launch (start us, length us, event | category | flops | bytes accessed | tf_op | source)
XLA Modules:
  0.0 161.5 jit_solution(407017061728834318)
XLA Ops:
  0.6 157.2 %shard_map.77 = (f32[1,160,768]{2,1,0:T(8,128)}, f32[1,48,2560]{2,1,0:T(8,128)}) custom-call(s32[6,128]{1,0:T(8,128)} %bitcast.2, f32[6,128]{1,0:T(8,128)} %bitcast.3, bf16[128,2560]{1,0:T(8,128)(2,1)} %tok.1, bf16[128,2560]{1,0:T(8,128)(2,1)} %cot.1, bf16[1,2560,768]{2,1,0:T(8,128)(2,1)} %win_hbm.1, bf16[1,768,2560]{2,1,0:T(8,128)(2,1)} %wout_hbm.1), custom_call_target="tpu_custom_call" | custom-call | tf_op jit(solution)/shard_map/pallas_call | solution.py:255
  157.8 1.8 %copy.10 = f32[1,160,768]{2,1,0:T(8,128)} copy(f32[1,160,768]{2,1,0:T(8,128)} %get-tuple-element.4) | data formatting | bytes 983040
  159.7 1.8 %copy.11 = f32[1,48,2560]{2,1,0:T(8,128)} copy(f32[1,48,2560]{2,1,0:T(8,128)} %get-tuple-element.5) | data formatting | bytes 983040

commit v3 on v1

v3 whole, which is shorter than its diff:
```python
import functools

import jax
import jax.numpy as jnp
from jax import lax
from jax.experimental import pallas as pl
from jax.experimental.pallas import tpu as pltpu
from jax.sharding import PartitionSpec as P

MESH = pl.DeviceIdType.MESH
BF = jnp.bfloat16
F32 = jnp.float32
NEX = 16
HALF = 8
CAP = 40
ROWS = NEX * CAP
COT_SPLIT = 5
TOK_SPLIT = 2
IN_UNITS = 6
RING = 8
OUT_MODES = "zzzzy"
IN_MODES = "zzzyyy"
PLAN = (
    0, 10, 30, 1, 11, 30, 31, 2, 12, 30, 31, 32, 3, 30, 13, 31, 32, 33, 4, 14, 20, 21, 22, 31, 32,
    33, 40, 41, 42, 32, 34, 33, 40, 41, 42, 34, 43, 33, 40, 41, 44, 42, 43, 34, 40, 41, 44, 45, 42,
    43, 34, 45, 44, 43, 34, 45, 44, 43, 45, 44, 45,
)


def silu_slope(values):
    sigma = jax.nn.sigmoid(values)
    return sigma * (1.0 + values * (1.0 - sigma))


def mm(a, b, dims):
    return lax.dot_general(a, b, (dims, ((), ())), preferred_element_type=F32)


class Sums:
    def __init__(self, modes, cols, out, refs, place):
        self.modes, self.cols, self.out = modes, cols, out
        self.part, self.land, self.ysend, self.yrecv, self.ssem, self.rsem, self.yss, self.yrs = refs
        self.yl, self.z, self.up, self.down, self.side = place
        self.todo = {}

    def hops(self, u, direction):
        return range(1, 5) if self.modes[u] == "z" or u % 2 == direction else range(2, 5)

    def target(self, direction, s):
        return lax.rem(self.z + (5 - s if direction == 0 else s - 5) + RING, RING)

    def piece(self, u, direction, s):
        if self.modes[u] == "y":
            return self.yl
        if s == 1:
            return 1 - self.yl if direction == 0 else self.yl
        return slice(None)

    def remote(self, src, dst, ssem, rsem, device):
        return pltpu.make_async_remote_copy(
            src_ref=src, dst_ref=dst, send_sem=ssem, recv_sem=rsem, device_id=device, device_id_type=MESH)

    def hop(self, u, direction, s):
        slot = direction * 4 + s - 1
        row = self.piece(u, direction, s)
        return self.remote(
            self.part.at[u, row, self.target(direction, s)], self.land.at[u, row, slot],
            self.ssem.at[u], self.rsem.at[u, slot], self.up if direction == 0 else self.down)

    def step(self, u, s):
        for direction in (0, 1):
            if s not in self.hops(u, direction):
                continue
            if s - 1 in self.hops(u, direction):
                self.hop(u, direction, s - 1).wait_recv()
                row = self.piece(u, direction, s - 1)
                at = self.target(direction, s)
                got = self.land[u, row, direction * 4 + s - 2].astype(F32)
                self.part[u, row, at] = (self.part[u, row, at].astype(F32) + got).astype(BF)
            self.hop(u, direction, s).start()

    def ycopy(self, u):
        if self.modes[u] == "y":
            source, target = self.part.at[u, 1 - self.yl], self.land.at[u, self.yl]
        else:
            source, target = self.ysend.at[u], self.yrecv.at[u]
        return self.remote(source, target, self.yss.at[u], self.yrs.at[u], self.side)

    def begin(self, u):
        if self.modes[u] == "y":
            self.ycopy(u).start()
            self.todo[u] = ["add", 2, 3, 4, "end"]
        else:
            self.step(u, 1)
            self.todo[u] = [2, 3, 4, "end"]

    def advance(self, u):
        stage = self.todo[u].pop(0)
        with jax.named_scope(f"{stage}u{u}{self.modes[u]}{self.cols}"):
            if stage == "add":
                self.ycopy(u).wait_recv()
                got = self.land[u, 1 - self.yl].astype(F32)
                self.part[u, self.yl] = (self.part[u, self.yl].astype(F32) + got).astype(BF)
                self.step(u, 1)
            elif stage == "end":
                self.end(u)
            else:
                self.step(u, stage)

    def end(self, u):
        span = slice(self.cols * u, self.cols * (u + 1))
        for direction in (0, 1):
            self.hop(u, direction, 4).wait_recv()
        for row in (1 - self.yl, self.yl) if self.modes[u] == "z" else (self.yl,):
            total = self.part[u, row, self.z].astype(F32)
            total += self.land[u, row, 3].astype(F32) + self.land[u, row, 7].astype(F32)
            if self.modes[u] == "z" and row is not self.yl:
                self.ysend[u] = total.astype(BF)
                self.ycopy(u).start()
            else:
                self.out[0, :, span] = total

    def finish(self, u):
        assert not self.todo[u]
        span = slice(self.cols * u, self.cols * (u + 1))
        copy = self.ycopy(u)
        copy.wait_send()
        sent = slice(0, RING - 1)
        if self.modes[u] == "z":
            copy.wait_recv()
            self.out[0, :, span] += self.yrecv[u].astype(F32)
            all_sent = self.part.at[u, :, sent]
        else:
            all_sent = self.part.at[u, 0, sent]
        self.remote(all_sent, all_sent, self.ssem.at[u], self.rsem.at[u, 0], self.up).wait_send()


def kernel(routing, gates, tok, cot, win_hbm, wout_hbm, gin, gout,
           win, wout, stok, scot, rtok, rcot, tokf, cotb, onehot, prt, pgt, ptok, pcot, slope, back, hid, pgrad,
           po, pi, lo, li, yso, yro, ysi, yri,
           wsem, lsem, ps, pr, ts, tr, cs, cr, zos, zor, zis, zir, yos, yor, yis, yir):
    me = lax.axis_index("expert")
    dp = lax.axis_index("dp")
    yh = me // HALF
    r = lax.rem(me, HALF)
    yl = dp // RING
    z = lax.rem(dp, RING)
    up = {"dp": yl * RING + lax.rem(z + 1, RING)}
    down = {"dp": yl * RING + lax.rem(z + RING - 1, RING)}
    side = {"dp": (1 - yl) * RING + z}
    partner = {"expert": (1 - yh) * HALF + r}
    row = [lax.rem(r + o, HALF) for o in range(HALF)]
    width = tok.shape[1]
    toks = tok.shape[0]
    ff = win.shape[1]
    cblock = width // COT_SPLIT
    iblock = ff // IN_UNITS
    place = (yl, z, up, down, side)
    so = Sums(OUT_MODES, cblock, gout, (po, lo, yso, yro, zos, zor, yos, yor), place)
    si = Sums(IN_MODES, iblock, gin, (pi, li, ysi, yri, zis, zir, yis, yir), place)

    weights = []
    for i, (src, dst) in enumerate(((win_hbm, win), (wout_hbm, wout))):
        copy = pltpu.make_async_copy(src.at[0], dst, wsem.at[i])
        copy.start()
        weights.append(copy)

    barrier = pltpu.get_barrier_semaphore()
    peers = [{"expert": yh * HALF + t} for t in row[1:]] + [partner, up, down, side]
    for peer in peers:
        pl.semaphore_signal(barrier, inc=1, device_id=peer, device_id_type=MESH)

    def slots(j, routes, values):
        expert = lax.broadcasted_iota(jnp.int32, (HALF, toks), 0) + yh * HALF
        member = jnp.zeros((HALF, toks), F32)
        weight = jnp.zeros((HALF, toks), F32)
        for k in range(routes.shape[0]):
            hit = routes[k : k + 1, :] == expert
            member = jnp.where(hit, 1.0, member)
            weight = jnp.where(hit, values[k : k + 1, :], weight)
        first = lax.broadcasted_iota(jnp.int32, (toks, toks), 0)
        before = first < lax.broadcasted_iota(jnp.int32, (toks, toks), 1)
        rank = mm(member.astype(BF), jnp.where(before, 1.0, 0.0).astype(BF), ((1,), (0,)))
        rank = jnp.where(member > 0.0, rank, -1.0)
        spot = lax.broadcasted_iota(jnp.int32, (HALF, CAP, toks), 1).astype(F32)
        match = spot == rank[:, None, :]
        onehot[j] = jnp.where(match, 1.0, 0.0).reshape(HALF * CAP, toks).astype(BF)
        scale = jnp.sum(jnp.where(match, weight[:, None, :], 0.0), axis=2, keepdims=True)
        return scale.reshape(HALF * CAP, 1)

    def gather(j, source, send, scale, start, stop):
        for c in range(start, stop, 256):
            value = mm(onehot[j], source[:, c : c + 256], ((1,), (0,)))
            if scale is not None:
                value = value * scale
            send[j, :, :, c : c + 256] = value.reshape(HALF, CAP, 256).astype(BF)

    own_gate = slots(0, routing, gates)
    gather(0, tok, stok, None, 0, width)
    with jax.named_scope("barrier"):
        pl.semaphore_wait(barrier, len(peers))

    given = []
    half = width // 2
    for i, (src, dst) in enumerate((
            (routing, prt), (gates, pgt), (tok.at[:, :half], ptok.at[:, :half]), (tok.at[:, half:], ptok.at[:, half:]),
            (cot, pcot))):
        copy = pltpu.make_async_remote_copy(
            src_ref=src, dst_ref=dst, send_sem=ps.at[i], recv_sem=pr.at[i], device_id=partner, device_id_type=MESH)
        copy.start()
        given.append(copy)

    tok_copies, cot_copies = [], []
    thalf = width // TOK_SPLIT

    def spread(send, recv, ssem, rsem, osem):
        for o in range(1, HALF):
            pltpu.make_async_remote_copy(
                src_ref=send(row[o]), dst_ref=recv(r), send_sem=ssem, recv_sem=rsem,
                device_id={"expert": yh * HALF + row[o]}, device_id_type=MESH).start()
        own = pltpu.make_async_copy(send(r), recv(r), osem)
        own.start()
        some = slice(0, HALF - 1)
        whole = pltpu.make_async_remote_copy(
            src_ref=send(some), dst_ref=recv(some), send_sem=ssem, recv_sem=rsem,
            device_id=partner, device_id_type=MESH)
        return whole, own

    def send_tok(j, k):
        span = pl.ds(k * thalf, thalf)
        i = j * TOK_SPLIT + k
        tok_copies.append(spread(
            lambda t: stok.at[j, t, :, span], lambda t: rtok.at[j, t, :, span], ts.at[i], tr.at[i], lsem.at[i]))

    def send_cot(b):
        span = pl.ds(b * cblock, cblock)
        cot_copies.append(spread(
            lambda t: scot.at[:, t, :, span], lambda t: rcot.at[:, t, :, span], cs.at[b], cr.at[b],
            lsem.at[2 * TOK_SPLIT + b]))

    def arrived(entry):
        with jax.named_scope("arrived"):
            whole, own = entry
            own.wait()
            whole.wait_recv()

    for k in range(TOK_SPLIT):
        send_tok(0, k)
    gather(0, cot, scot, own_gate, 0, width)
    with jax.named_scope("pmeta"):
        given[0].wait_recv()
        given[1].wait_recv()
    partner_gate = slots(1, prt, pgt)
    for k in range(TOK_SPLIT):
        with jax.named_scope("ptok"):
            given[2 + k].wait_recv()
        gather(1, ptok, stok, None, k * thalf, (k + 1) * thalf)
        send_tok(1, k)
    with jax.named_scope("pcot"):
        given[4].wait_recv()
    gather(1, pcot, scot, partner_gate, 0, width)
    send_cot(0)

    weights[0].wait()
    for j in (0, 1):
        for k in range(TOK_SPLIT):
            arrived(tok_copies[j * TOK_SPLIT + k])
        if j == 1:
            send_cot(1)
        rows = slice(j * HALF * CAP, (j + 1) * HALF * CAP)
        for t in range(0, HALF, 2):
            at = (j * HALF + t) * CAP
            tokf[at : at + 2 * CAP, :] = rtok[j, t : t + 2].astype(F32).reshape(2 * CAP, width).astype(BF)
        for n in range(0, ff, 256):
            value = mm(tokf[rows, :], win[:, n : n + 256], ((1,), (0,)))
            hid[rows, n : n + 256] = (value * jax.nn.sigmoid(value)).astype(BF)
            slope[rows, n : n + 256] = silu_slope(value)
    weights[1].wait()

    def out_block(b):
        arrived(cot_copies[b])
        if b + 2 < COT_SPLIT:
            send_cot(b + 2)
        span = slice(b * cblock, (b + 1) * cblock)
        for j in (0, 1):
            for t in range(0, HALF, 2):
                at = (j * HALF + t) * CAP
                cotb[at : at + 2 * CAP, :] = rcot[j, t : t + 2, :, span].astype(F32).reshape(2 * CAP, cblock).astype(BF)
        for m in range(0, ff, 384):
            value = mm(hid[:, m : m + 384], cotb[...], ((0,), (0,)))
            po[b, m // 384] = value.reshape(8, 48, cblock).astype(BF)
        so.begin(b)

    def back_block(b):
        span = slice(b * cblock, (b + 1) * cblock)
        for n in range(0, ff, 256):
            value = mm(cotb[...], wout[n : n + 256, span], ((1,), (1,)))
            if b > 0:
                value += back[:, n : n + 256]
            if b < COT_SPLIT - 1:
                back[:, n : n + 256] = value
            else:
                pgrad[:, n : n + 256] = (value * slope[:, n : n + 256]).astype(BF)

    def in_block(n):
        with jax.named_scope(f"part_in{n}"):
            for m in range(0, width, 640):
                value = mm(tokf[:, m : m + 640], pgrad[:, n * 256 : (n + 1) * 256], ((0,), (0,)))
                value = value.reshape(4, 160, 256).astype(BF)
                for i in (0, 1):
                    pi[2 * n + i, m // 1280, m % 1280 // 160 : m % 1280 // 160 + 4] = value[:, :, i * 128 : (i + 1) * 128]
        si.begin(2 * n)
        si.begin(2 * n + 1)

    todo = (out_block, back_block, in_block, so.advance, si.advance)
    for entry in PLAN:
        todo[entry // 10](entry % 10)
    for b in range(COT_SPLIT):
        so.finish(b)
    for u in range(IN_UNITS):
        si.finish(u)
    for whole, _ in tok_copies + cot_copies:
        whole.wait_send()
    for copy in given:
        copy.wait_send()


def body(tokens, routing, gates, cotangent, w_in, w_out):
    toks, width = tokens.shape
    ff = w_in.shape[2]
    cblock = width // COT_SPLIT
    iblock = ff // IN_UNITS
    vmem = pl.BlockSpec(memory_space=pltpu.VMEM)
    hbm = pl.BlockSpec(memory_space=pl.ANY)
    dma = pltpu.SemaphoreType.DMA
    topk = routing.shape[1]
    slot = (2, HALF, CAP, width)
    return pl.pallas_call(
        kernel,
        out_shape=(
            jax.ShapeDtypeStruct((1, width // 16, ff), F32),
            jax.ShapeDtypeStruct((1, ff // 16, width), F32),
        ),
        in_specs=[vmem, vmem, vmem, vmem, hbm, hbm],
        out_specs=(vmem, vmem),
        scratch_shapes=[
            pltpu.VMEM((width, ff), BF), pltpu.VMEM((ff, width), BF),
            pltpu.VMEM(slot, BF), pltpu.VMEM(slot, BF), pltpu.VMEM(slot, BF), pltpu.VMEM(slot, BF),
            pltpu.VMEM((ROWS, width), BF), pltpu.VMEM((ROWS, cblock), BF), pltpu.VMEM((2, ROWS // 2, toks), BF),
            pltpu.VMEM((topk, toks), jnp.int32), pltpu.VMEM((topk, toks), F32),
            pltpu.VMEM((toks, width), BF), pltpu.VMEM((toks, width), BF),
            pltpu.VMEM((ROWS, ff), F32), pltpu.VMEM((ROWS, ff), F32),
            pltpu.VMEM((ROWS, ff), BF), pltpu.VMEM((ROWS, ff), BF),
            pltpu.VMEM((COT_SPLIT, 2, RING, ff // 16, cblock), BF), pltpu.VMEM((IN_UNITS, 2, RING, width // 16, iblock), BF),
            pltpu.VMEM((COT_SPLIT, 2, RING, ff // 16, cblock), BF), pltpu.VMEM((IN_UNITS, 2, RING, width // 16, iblock), BF),
            pltpu.VMEM((COT_SPLIT, ff // 16, cblock), BF), pltpu.VMEM((COT_SPLIT, ff // 16, cblock), BF),
            pltpu.VMEM((IN_UNITS, width // 16, iblock), BF), pltpu.VMEM((IN_UNITS, width // 16, iblock), BF),
            dma((2,)), dma((2 * TOK_SPLIT + COT_SPLIT,)), dma((5,)), dma((5,)),
            dma((2 * TOK_SPLIT,)), dma((2 * TOK_SPLIT,)), dma((COT_SPLIT,)), dma((COT_SPLIT,)),
            dma((COT_SPLIT,)), dma((COT_SPLIT, 8)), dma((IN_UNITS,)), dma((IN_UNITS, 8)),
            dma((COT_SPLIT,)), dma((COT_SPLIT,)), dma((IN_UNITS,)), dma((IN_UNITS,)),
        ],
        compiler_params=pltpu.CompilerParams(
            collective_id=0, has_side_effects=True, vmem_limit_bytes=62 * 1024 * 1024
        ),
    )(routing.T, gates.T, tokens, cotangent, w_in, w_out)


def solution(mesh):
    rows = P(("dp", "expert"), None)
    in_specs = (rows, rows, rows, rows, P("expert", None, None), P("expert", None, None))
    out_specs = (P("expert", "dp", None), P("expert", "dp", None))
    return jax.shard_map(body, mesh=mesh, in_specs=in_specs, out_specs=out_specs, check_vma=False)
```

time: 299 us -> 135 us (0.45)
  waiting for transfers between devices: 216 us -> 0 us
  Pallas kernels: 0 us -> 130 us
  matrix products: 26.4 us -> 0 us
  local copies, waits for them, and re-layouts: 17.9 us -> 3.68 us
  between operations: 14.2 us -> 0.64 us
  starting transfers between devices: 12.2 us -> 0 us
  other arithmetic: 10.4 us -> 0 us
    reduce_scatter x2 -> x0, waiting for transfers between devices: 147 us -> none  [the longest x1 77.9 us: body(): lax.psum_scatter(rounded_in, 'dp', scatter_dimension=0, tiled=True)]
    pallas_call x0 -> x1, Pallas kernels: none -> 130 us  [body(): pl.pallas_call(kernel, out_shape=(jax.ShapeDtypeStruct((1, width // 16, f...]
    all_to_all x2 -> x0, waiting for transfers between devices: 69.2 us -> none  [the longest x1 37 us: body(): lax.all_to_all(sent_grads, 'expert', split_axis=0, concat_axis=0, tiled=T...]
    dot_general x4 -> x0, matrix products: 26.4 us -> none  [the longest x1 7.2 us: outer_sums(): lax.dot_general(rows_in, pre_grad, (((0,), (0,)), ((), ())), preferred_el...]
    all_to_all x2 -> x0, starting transfers between devices: 12 us -> none  [the longest x1 6.31 us: body(): lax.all_to_all(sent_inputs, 'expert', split_axis=0, concat_axis=0, tiled=...]
    gather x3 -> x0, local copies, waits for them, and re-layouts: 11.5 us -> none  [the longest x1 4.36 us: body(): padded_cots[token_of].astype(jnp.float32)]
    convert_element_type x2 -> x0, other arithmetic: 4.28 us -> none  [the longest x1 4.27 us: body(): sent_grads = (padded_cots[token_of].astype(jnp.float32) * padded_gates[sl...]
    broadcast_in_dim x2 -> x0, other arithmetic: 3.51 us -> none  [body(): return (sum_in[None], sum_out[None])]
  transfers between devices with their start and end apart: 4 -> 0, of which waited for: 4 -> 0; matrix products, arithmetic and copies ran while one was open for 11% -> 0% of each run, Pallas kernels for 0% -> 0%
where the time goes in v3:
time: 135 us; the launch traced here: 134 us
  Pallas kernels  130 us (96%)
  local copies, waits for them, and re-layouts  3.68 us (3%)
    pallas_call x1, Pallas kernels, body(): pl.pallas_call(kernel, out_shape=(jax.ShapeDtypeStruct((1, width // 16, f...  130 us
    unnamed x2, local copies, waits for them, and re-layouts  3.68 us

profile of v3, /device:TPU:8, one launch (start us, length us, event | category | flops | bytes accessed | tf_op | source)
XLA Modules:
  0.0 134.2 jit_solution(8025038781944607542)
XLA Ops:
  0.6 129.9 %shard_map.77 = (f32[1,160,768]{2,1,0:T(8,128)}, f32[1,48,2560]{2,1,0:T(8,128)}) custom-call(s32[6,128]{1,0:T(8,128)} %bitcast.2, f32[6,128]{1,0:T(8,128)} %bitcast.3, bf16[128,2560]{1,0:T(8,128)(2,1)} %tok.1, bf16[128,2560]{1,0:T(8,128)(2,1)} %cot.1, bf16[1,2560,768]{2,1,0:T(8,128)(2,1)} %win_hbm.1, bf16[1,768,2560]{2,1,0:T(8,128)(2,1)} %wout_hbm.1), custom_call_target="tpu_custom_call" | custom-call | tf_op jit(solution)/shard_map/pallas_call | solution.py:338
  130.5 1.8 %copy.10 = f32[1,160,768]{2,1,0:T(8,128)} copy(f32[1,160,768]{2,1,0:T(8,128)} %get-tuple-element.4) | data formatting | bytes 983040
  132.4 1.8 %copy.11 = f32[1,48,2560]{2,1,0:T(8,128)} copy(f32[1,48,2560]{2,1,0:T(8,128)} %get-tuple-element.5) | data formatting | bytes 983040

commit v4 on v3

--- a/solution.py
+++ b/solution.py
@@ -325,6 +325,19 @@
         copy.wait_send()
 
 
+def hand_over(a_in, b_in, a_out, b_out, a_buf, b_buf, sem):
+    trips = []
+    for i, (src, buf, dst) in enumerate(((a_in, a_buf, a_out), (b_in, b_buf, b_out))):
+        into = pltpu.make_async_copy(src, buf, sem.at[2 * i])
+        into.start()
+        trips.append((into, pltpu.make_async_copy(buf, dst, sem.at[2 * i + 1])))
+    for into, back in trips:
+        into.wait()
+        back.start()
+    for _, back in trips:
+        back.wait()
+
+
 def body(tokens, routing, gates, cotangent, w_in, w_out):
     toks, width = tokens.shape
     ff = w_in.shape[2]
@@ -335,7 +348,7 @@
     dma = pltpu.SemaphoreType.DMA
     topk = routing.shape[1]
     slot = (2, HALF, CAP, width)
-    return pl.pallas_call(
+    sums = pl.pallas_call(
         kernel,
         out_shape=(
             jax.ShapeDtypeStruct((1, width // 16, ff), F32),
@@ -364,6 +377,13 @@
             collective_id=0, has_side_effects=True, vmem_limit_bytes=62 * 1024 * 1024
         ),
     )(routing.T, gates.T, tokens, cotangent, w_in, w_out)
+    return pl.pallas_call(
+        hand_over,
+        out_shape=tuple(jax.ShapeDtypeStruct(x.shape, x.dtype) for x in sums),
+        in_specs=[hbm, hbm],
+        out_specs=(hbm, hbm),
+        scratch_shapes=[pltpu.VMEM(x.shape, x.dtype) for x in sums] + [dma((4,))],
+    )(*sums)
 
 
 def solution(mesh):

time: 135 us -> 133 us (0.985)
  local copies, waits for them, and re-layouts: 3.68 us -> 0 us
  Pallas kernels: 130 us -> 132 us
    unnamed x2 -> x0, local copies, waits for them, and re-layouts: 3.68 us -> none
    pallas_call x0 -> x1, Pallas kernels: none -> 2 us  [body(): pl.pallas_call(hand_over, out_shape=tuple((jax.ShapeDtypeStruct(x.shape,...]
where the time goes in v4:
time: 133 us
  Pallas kernels  132 us (99%)
    pallas_call x1, Pallas kernels, body(): pl.pallas_call(kernel, out_shape=(jax.ShapeDtypeStruct((1, width // 16, f...  130 us

profile of v4, /device:TPU:8, one launch (start us, length us, event | category | flops | bytes accessed | tf_op | source)
XLA Modules:
  0.0 132.7 jit_solution(11416208577715361768)
XLA Ops:
  0.6 129.9 %shard_map.77 = (f32[1,160,768]{2,1,0:T(8,128)}, f32[1,48,2560]{2,1,0:T(8,128)}) custom-call(s32[6,128]{1,0:T(8,128)} %bitcast.2, f32[6,128]{1,0:T(8,128)} %bitcast.3, bf16[128,2560]{1,0:T(8,128)(2,1)} %tok.1, bf16[128,2560]{1,0:T(8,128)(2,1)} %cot.1, bf16[1,2560,768]{2,1,0:T(8,128)(2,1)} %win_hbm.1, bf16[1,768,2560]{2,1,0:T(8,128)(2,1)} %wout_hbm.1), custom_call_target="tpu_custom_call" | custom-call | tf_op jit(solution)/shard_map/pallas_call | solution.py:351
  130.5 2.0 %shard_map.78 = (f32[1,160,768]{2,1,0:T(8,128)}, f32[1,48,2560]{2,1,0:T(8,128)}) custom-call(f32[1,160,768]{2,1,0:T(8,128)} %get-tuple-element.4.a_in, f32[1,48,2560]{2,1,0:T(8,128)} %get-tuple-element.5.b_in), custom_call_target="tpu_custom_call" | custom-call | tf_op jit(solution)/shard_map/pallas_call | solution.py:380

commit v5 on v4

--- a/solution.py
+++ b/solution.py
@@ -18,12 +18,12 @@
 TOK_SPLIT = 2
 IN_UNITS = 6
 RING = 8
-OUT_MODES = "zzzzy"
+OUT_MODES = "zzzzz"
 IN_MODES = "zzzyyy"
 PLAN = (
     0, 10, 30, 1, 11, 30, 31, 2, 12, 30, 31, 32, 3, 30, 13, 31, 32, 33, 4, 14, 20, 21, 22, 31, 32,
-    33, 40, 41, 42, 32, 34, 33, 40, 41, 42, 34, 43, 33, 40, 41, 44, 42, 43, 34, 40, 41, 44, 45, 42,
-    43, 34, 45, 44, 43, 34, 45, 44, 43, 45, 44, 45,
+    33, 34, 40, 41, 42, 32, 33, 43, 34, 40, 41, 42, 44, 33, 43, 34, 40, 45, 41, 42, 44, 43, 34, 40,
+    45, 41, 42, 44, 43, 45, 44, 43, 45, 44, 45,
 )
 
 

time: 133 us -> 136 us (1.023)
  Pallas kernels: 132 us -> 134 us
    pallas_call x1, Pallas kernels: 130 us -> 132 us  [body(): pl.pallas_call(kernel, out_shape=(jax.ShapeDtypeStruct((1, width // 16, f...]
where the time goes in v5:
time: 136 us; the launch traced here: 135 us
  Pallas kernels  134 us (99%)
    pallas_call x1, Pallas kernels, body(): pl.pallas_call(kernel, out_shape=(jax.ShapeDtypeStruct((1, width // 16, f...  132 us

profile of v5, /device:TPU:8, one launch (start us, length us, event | category | flops | bytes accessed | tf_op | source)
XLA Modules:
  0.0 134.6 jit_solution(13596779244917524521)
XLA Ops:
  0.6 131.8 %shard_map.77 = (f32[1,160,768]{2,1,0:T(8,128)}, f32[1,48,2560]{2,1,0:T(8,128)}) custom-call(s32[6,128]{1,0:T(8,128)} %bitcast.2, f32[6,128]{1,0:T(8,128)} %bitcast.3, bf16[128,2560]{1,0:T(8,128)(2,1)} %tok.1, bf16[128,2560]{1,0:T(8,128)(2,1)} %cot.1, bf16[1,2560,768]{2,1,0:T(8,128)(2,1)} %win_hbm.1, bf16[1,768,2560]{2,1,0:T(8,128)(2,1)} %wout_hbm.1), custom_call_target="tpu_custom_call" | custom-call | tf_op jit(solution)/shard_map/pallas_call | solution.py:351
  132.5 2.0 %shard_map.78 = (f32[1,160,768]{2,1,0:T(8,128)}, f32[1,48,2560]{2,1,0:T(8,128)}) custom-call(f32[1,160,768]{2,1,0:T(8,128)} %get-tuple-element.4.a_in, f32[1,48,2560]{2,1,0:T(8,128)} %get-tuple-element.5.b_in), custom_call_target="tpu_custom_call" | custom-call | tf_op jit(solution)/shard_map/pallas_call | solution.py:380
